TPU v7x, 256 devices: a whole 4x4x8 slice. The times are simulated.
256 devices in a mesh: dp: 32 (over y, z_lo, core), seq: 8 (over z_hi, x).
Axes of the slice: x: 4, y: 4, z: 8 (z_hi: 2, z_lo: 4; z = z_hi * 4 + z_lo), core: 2. Of those that a mesh axis runs over, the one named last changes fastest.
Arguments:
- stream_in: bfloat16 [32, 1024, 768], P('dp', 'seq'), may hold values from -30 to 30
- queries: bfloat16 [32, 1024, 768], P('dp', 'seq'), may hold values from -5.6 to 5.6
- key_rows: bfloat16 [32, 1024, 768], P('dp', 'seq'), may hold values from -5.6 to 5.6
- value_rows: bfloat16 [32, 1024, 768], P('dp', 'seq'), may hold values from -6 to 6
- conv_weight: bfloat16 [768, 5, 768], P('dp'), may hold values from -0.09375 to 0.09375
- cotangent: bfloat16 [32, 1024, 768], P('dp', 'seq'), may hold values from -6 to 6
Outputs:
- grad_stream: bfloat16 [32, 1024, 768], P('dp', 'seq')
- grad_queries: bfloat16 [32, 1024, 768], P('dp', 'seq')
- grad_keys: bfloat16 [32, 1024, 768], P('dp', 'seq')
- grad_values: bfloat16 [32, 1024, 768], P('dp', 'seq')
- grad_weight: float32 [768, 5, 768], P('dp')
All inputs are finite; a program needn't handle non-finite values.
Results may differ from a plain program's by a relative error of at most 0.017.
Values may be sent and summed in bfloat16 or wider, within the bound.
A program may use at most 128 MiB of HBM per device.

v0:
```python
import jax
import jax.numpy as jnp
from jax import lax
from jax.sharding import PartitionSpec as P

HEADS = 8
HEAD_DIM = 96
TAPS = 5


def padded(block, sides, width):
    for axis, dim in sides:
        count = lax.axis_size(axis)
        forward = [(i, i + 1) for i in range(count - 1)]
        backward = [(target, source) for source, target in forward]
        low = lax.ppermute(
            lax.slice_in_dim(block, block.shape[dim] - width, None, axis=dim), axis, forward
        )
        high = lax.ppermute(lax.slice_in_dim(block, 0, width, axis=dim), axis, backward)
        block = jnp.concatenate([low, block, high], axis=dim)
    return block


def activate(stream):
    square = jnp.mean(stream * stream, axis=-1, keepdims=True)
    return jax.nn.gelu(stream * lax.rsqrt(square + 1e-06), approximate=True)


def attend_forward(query, keys, values, scale):
    scores = jnp.einsum("rhd,nhd->hrn", query, keys, preferred_element_type=jnp.float32) * scale
    top = jnp.max(scores, axis=-1, keepdims=True)
    expo = jnp.exp(scores - top)
    total = jnp.sum(expo, axis=-1, keepdims=True)
    expo_b = expo.astype(jnp.bfloat16)
    attended = jnp.einsum("hrn,nhd->rhd", expo_b, values, preferred_element_type=jnp.float32)
    attended = attended / jnp.transpose(total, (1, 0, 2))
    return (expo, total, attended)


def attend_back(keys, values, expo, total, attended, dout, scale):
    probs = expo / total
    probs_b = probs.astype(jnp.bfloat16)
    delta = jnp.transpose(jnp.sum(dout.astype(jnp.float32) * attended, axis=-1), (1, 0))[:, :, None]
    dprob = jnp.einsum("rhd,nhd->hrn", dout, values, preferred_element_type=jnp.float32)
    dscore = (probs * (dprob - delta)).astype(jnp.bfloat16)
    grad_query = (
        jnp.einsum("hrn,nhd->rhd", dscore, keys, preferred_element_type=jnp.float32) * scale
    )
    return (dscore, probs_b, grad_query)


def body(stream_in, queries, key_rows, value_rows, conv_weight, cotangent):
    rows = queries.shape[1]
    channels = queries.shape[2]
    dp_count = lax.axis_size("dp")
    seq_count = lax.axis_size("seq")
    length = rows * seq_count
    scale = HEAD_DIM ** (-0.5)
    half = TAPS // 2
    query_local = queries[0].reshape(rows, HEADS, HEAD_DIM)
    keys_all, values_all = (
        lax.all_gather(key_rows, "seq", axis=1, tiled=True),
        lax.all_gather(value_rows, "seq", axis=1, tiled=True),
    )
    keys_full = keys_all[0].reshape(length, HEADS, HEAD_DIM)
    values_full = values_all[0].reshape(length, HEADS, HEAD_DIM)
    expo, total, attended = attend_forward(query_local, keys_full, values_full, scale)
    attended_flat = attended.reshape(rows, channels)
    stream = (stream_in[0].astype(jnp.float32) + attended_flat).astype(jnp.bfloat16)
    hidden, pullback = jax.vjp(activate, stream.astype(jnp.float32))
    hidden_b = hidden.astype(jnp.bfloat16)
    full_weight = lax.all_gather(conv_weight, "dp", axis=0, tiled=True)
    extended = padded(jnp.stack([hidden_b, cotangent[0]]), (("seq", 1),), half)
    hid_ext = extended[0]
    cot_ext = extended[1]
    cot_local = cotangent[0]
    windows = jnp.stack([hid_ext[tap : tap + rows] for tap in range(TAPS)], axis=1).reshape(
        rows, TAPS * channels
    )
    norm_factor = 1.0 / jnp.sqrt(jnp.float32(dp_count * length))
    owned = lax.psum_scatter(
        jnp.einsum("to,tk->ok", cot_local, windows, preferred_element_type=jnp.float32),
        "dp",
        scatter_dimension=0,
        tiled=True,
    )
    summed = lax.psum(owned, "seq")
    grad_weight = (summed * norm_factor).reshape(summed.shape[0], TAPS, channels)
    back = jnp.zeros((rows, channels), jnp.float32)
    for tap in range(TAPS):
        start = 2 * half - tap
        back = back + jnp.dot(
            cot_ext[start : start + rows],
            full_weight[:, tap, :],
            preferred_element_type=jnp.float32,
        )
    grad_stream = (cot_local.astype(jnp.float32) + pullback(back)[0]).astype(jnp.bfloat16)
    dout = grad_stream.reshape(rows, HEADS, HEAD_DIM)
    dscore, probs_b, grad_query = attend_back(
        keys_full, values_full, expo, total, attended, dout, scale
    )
    key_part = (
        jnp.einsum("hrn,rhd->nhd", dscore, query_local, preferred_element_type=jnp.float32) * scale
    )
    value_part = jnp.einsum("hrn,rhd->nhd", probs_b, dout, preferred_element_type=jnp.float32)
    key_sum, value_sum = (
        lax.psum_scatter(
            key_part.reshape(1, length, channels).astype(jnp.bfloat16),
            "seq",
            scatter_dimension=1,
            tiled=True,
        ).astype(jnp.float32),
        lax.psum_scatter(
            value_part.reshape(1, length, channels).astype(jnp.bfloat16),
            "seq",
            scatter_dimension=1,
            tiled=True,
        ).astype(jnp.float32),
    )
    grad_queries = grad_query.reshape(1, rows, channels).astype(jnp.bfloat16)
    grad_keys = key_sum.astype(jnp.bfloat16)
    grad_values = value_sum.astype(jnp.bfloat16)
    return (grad_stream[None], grad_queries, grad_keys, grad_values, grad_weight)


def solution(mesh):
    in_specs = (
        P("dp", "seq", None),
        P("dp", "seq", None),
        P("dp", "seq", None),
        P("dp", "seq", None),
        P("dp", None, None),
        P("dp", "seq", None),
    )
    out_specs = (
        P("dp", "seq", None),
        P("dp", "seq", None),
        P("dp", "seq", None),
        P("dp", "seq", None),
        P("dp", None, None),
    )
    return jax.shard_map(body, mesh=mesh, in_specs=in_specs, out_specs=out_specs, check_vma=False)
```

profile of v0, /device:TPU:8, one launch (start us, length us, event | category | flops | bytes accessed | tf_op | source)
XLA Modules:
  0.0 708.1 jit_solution(6786424331102835818)
XLA Ops:
  9.4 1.1 copy.35
  10.5 1.1 copy.39
  11.7 71.0 %all-gather.4.cloned.1.call-done = bf16[1,1024,768]{2,1,0:T(8,128)(2,1)} async-done(((bf16[1,128,768]{2,1,0:T(8,128)(2,1)}), bf16[1,1024,768]{2,1,0:T(8,128)(2,1)}) %all-gather.4.cloned.1.call-update) | async-done | bytes 1572880 | tf_op jit(solution)/shard_map/all_gather | solution.py:62
  82.7 1.7 copy.36
  84.4 65.9 %all-gather.6.cloned.1.call-done = bf16[1,1024,768]{2,1,0:T(8,128)(2,1)} async-done(((bf16[1,128,768]{2,1,0:T(8,128)(2,1)}), bf16[1,1024,768]{2,1,0:T(8,128)(2,1)}) %all-gather.6.cloned.1.call-update) | async-done | bytes 1572880 | tf_op jit(solution)/shard_map/all_gather | solution.py:63
  150.2 2.6 copy.37
  154.6 1.7 copy-done.10
  157.7 3.0 collective-permute-start.1
  160.8 1.3 collective-permute-start
  162.1 4.2 collective-permute-done
  170.0 1.6 copy.44
  171.6 6.0 convolution_bitcast_fusion
  177.6 12.5 %copy.47 = f32[768,3840]{1,0:T(8,128)} copy(f32[768,3840]{0,1:T(8,128)} %convolution_bitcast_fusion) | data formatting | bytes 23592960
  190.4 23.2 %all-gather.8.cloned.1.call-done = bf16[768,5,768]{2,0,1:T(8,128)(2,1)} async-done(((bf16[24,5,768]{2,0,1:T(8,128)(2,1)}), bf16[768,5,768]{2,0,1:T(8,128)(2,1)}) %all-gather.8.cloned.1.call-update) | async-done | bytes 5898256 | tf_op jit(solution)/shard_map/all_gather | solution.py:72
  213.6 1.6 fusion.15
  215.2 1.6 convolution_add_fusion.3
  216.8 1.6 convolution_add_fusion.2
  218.4 1.6 convolution_add_fusion.1
  220.1 1.9 fusion.41
  222.3 145.9 %reduce-scatter.10.cloned.1.call-done = f32[24,3840]{1,0:T(8,128)} async-done(((f32[768,3840]{1,0:T(8,128)}), f32[24,3840]{1,0:T(8,128)}) %reduce-scatter.10.cloned.1.call-update) | async-done | bytes 368656
  368.3 2.8 copy.48
  371.2 4.6 fusion.9
  375.8 2.7 copy.43
  379.7 3.9 multiply_convert_fusion
  383.7 1.3 copy-done.1
  385.6 1.7 copy.42
  387.3 2.4 fusion.16
  390.5 124.3 %all-reduce.2.cloned.1.call-done = f32[24,3840]{0,1:T(8,128)} async-done(((f32[24,3840]{0,1:T(8,128)}), f32[24,3840]{0,1:T(8,128)}) %all-reduce.2.cloned.1.call-update) | async-done | bytes 368656 | tf_op jit(solution)/shard_map/psum | solution.py:87
  514.8 1.7 broadcast_multiply_fusion
  516.5 1.3 copy.46
  517.8 92.6 %reduce-scatter.8.cloned.1.call-done = bf16[1,128,768]{2,1,0:T(8,128)(2,1)} async-done(((bf16[1,1024,768]{2,1,0:T(8,128)(2,1)}), bf16[1,128,768]{2,1,0:T(8,128)(2,1)}) %reduce-scatter.8.cloned.1.call-update) | async-done | bytes 196624 | tf_op jit(solution)/shard_map/reduce_scatter | solution.py:113
  610.4 90.9 %reduce-scatter.6.cloned.1.call-done = bf16[1,128,768]{2,1,0:T(8,128)(2,1)} async-done(((bf16[1,1024,768]{2,1,0:T(8,128)(2,1)}), bf16[1,128,768]{2,1,0:T(8,128)(2,1)}) %reduce-scatter.6.cloned.1.call-update) | async-done | bytes 196624 | tf_op jit(solution)/shard_map/reduce_scatter | solution.py:107
  (62 shorter events, 12.4 us)
Async XLA Ops:
  7.2 75.5 %all-gather.4.cloned.1.call-start = ((), (), s32[]{:S(2)}) async-start(), calls=%async_computation.3 | async-start | bytes 1769472 | tf_op jit(solution)/shard_map/all_gather | solution.py:62
  7.9 142.3 %all-gather.6.cloned.1.call-start = ((), (), s32[]{:S(2)}) async-start(), calls=%async_computation.4 | async-start | bytes 1769472 | tf_op jit(solution)/shard_map/all_gather | solution.py:63
  8.6 205.0 %all-gather.8.cloned.1.call-start = ((), (), s32[]{:S(2)}) async-start(), calls=%async_computation.5 | async-start | bytes 6082560 | tf_op jit(solution)/shard_map/all_gather | solution.py:72
  9.4 358.9 %reduce-scatter.10.cloned.1.call-start = ((), (), s32[]{:S(2)}) async-start(), calls=%async_computation.9 | async-start | bytes 12165120
  10.5 142.3 %copy-start.7 = (bf16[1,128,768]{1,2,0:T(8,128)(2,1)}, bf16[1,128,768]{1,2,0:T(8,128)(2,1)S(1)}, u32[]{:S(2)}) copy-start(bf16[1,128,768]{1,2,0:T(8,128)(2,1)S(1)} %copy.35) | copy-start | bytes 589828
  153.7 3.6 copy-start
  153.7 2.6 copy-start.10
  156.2 1.2 copy-start.9
  156.2 1.4 copy-start.2
  157.7 4.4 collective-permute-start.1
  160.8 5.5 collective-permute-start
  166.4 2.9 copy-start.3
  166.4 2.9 copy-start.5
  190.1 23.5 %copy-start.6 = (bf16[2,130,768]{2,1,0:T(8,128)(2,1)S(1)}, bf16[2,130,768]{2,1,0:T(8,128)(2,1)}, u32[]{:S(2)}) copy-start(bf16[2,130,768]{2,1,0:T(8,128)(2,1)} %copy-done.5) | copy-start | bytes 1198084
  190.2 324.6 %all-reduce.2.cloned.1.call-start = ((), (), s32[]{:S(2)}) async-start(), calls=%async_computation.8 | async-start | bytes 3932160 | tf_op jit(solution)/shard_map/psum | solution.py:87
  190.4 28.0 %copy-start.4 = (bf16[2,130,768]{2,1,0:T(8,128)(2,1)S(1)}, bf16[2,130,768]{2,1,0:T(8,128)(2,1)}, u32[]{:S(2)}) copy-start(bf16[2,130,768]{2,1,0:T(8,128)(2,1)} %copy-done.3) | copy-start | bytes 1198084
  222.2 149.0 %copy-start.12 = (bf16[128,768]{1,0:T(8,128)(2,1)}, bf16[128,768]{1,0:T(8,128)(2,1)S(1)}, u32[]{:S(2)}) copy-start(bf16[128,768]{1,0:T(8,128)(2,1)S(1)} %fusion.43) | copy-start | bytes 589828
  222.3 148.8 %copy-start.13 = (bf16[128,768]{0,1:T(8,128)(2,1)}, bf16[128,768]{0,1:T(8,128)(2,1)S(1)}, u32[]{:S(2)}) copy-start(bf16[128,768]{0,1:T(8,128)(2,1)S(1)} %copy.41) | copy-start | bytes 589828
  371.1 239.3 %reduce-scatter.8.cloned.1.call-start = ((), (), s32[]{:S(2)}) async-start(), calls=%async_computation.7 | async-start | bytes 1769472 | tf_op jit(solution)/shard_map/reduce_scatter | solution.py:113
  375.8 3.9 copy-start.11
  378.5 322.8 %reduce-scatter.6.cloned.1.call-start = ((), (), s32[]{:S(2)}) async-start(), calls=%async_computation.6 | async-start | bytes 1769472 | tf_op jit(solution)/shard_map/reduce_scatter | solution.py:107
  379.7 5.3 copy-start.8
  383.7 1.3 copy-start.1
Sparse Core Ops, SparseCore 0:
  10.6 72.0 all-gather.3
  85.3 64.9 all-gather.5
  152.0 61.5 all-gather.7
  216.1 152.1 reduce-scatter.9
  371.2 143.4 all-reduce.1
  519.2 91.0 reduce-scatter.7
  615.0 86.2 reduce-scatter.5
where the time goes:
time: 709 us; the launch traced here: 708 us
  waiting for transfers between devices  620 us (87%)
  local copies, waits for them, and re-layouts  37.1 us (5%)
  matrix products  27.6 us (4%)
  between operations  14.4 us (2%)
    unnamed x8, waiting for transfers between devices  148 us
    psum x1, waiting for transfers between devices, body(): summed = lax.psum(owned, 'seq')  124 us
    reduce_scatter x1, waiting for transfers between devices, body(): lax.psum_scatter(value_part.reshape(1, length, channels).astype(jnp.bfloa...  92.6 us
    reduce_scatter x1, waiting for transfers between devices, body(): lax.psum_scatter(key_part.reshape(1, length, channels).astype(jnp.bfloat1...  90.9 us
    all_gather x1, waiting for transfers between devices, body(): lax.all_gather(key_rows, 'seq', axis=1, tiled=True)  71 us
    all_gather x1, waiting for transfers between devices, body(): lax.all_gather(value_rows, 'seq', axis=1, tiled=True)  65.9 us
    unnamed x37, local copies, waits for them, and re-layouts  24.5 us
    all_gather x1, waiting for transfers between devices, body(): full_weight = lax.all_gather(conv_weight, 'dp', axis=0, tiled=True)  23.2 us
  transfers between devices with their start and end apart: 9, of which 8 were waited for; matrix products, arithmetic and copies ran while one was open for 9% of the time, Pallas kernels for 0%

commit v1 on v0

--- a/solution.py
+++ b/solution.py
@@ -60,7 +60,9 @@
     query_local = queries[0].reshape(rows, HEADS, HEAD_DIM)
     keys_all, values_all = (
         lax.all_gather(key_rows, "seq", axis=1, tiled=True),
-        lax.all_gather(value_rows, "seq", axis=1, tiled=True),
+        jnp.concatenate(
+            lax.all_to_all(jnp.stack([value_rows] * lax.axis_size("seq")), "seq", 0, 0), axis=1
+        ),
     )
     keys_full = keys_all[0].reshape(length, HEADS, HEAD_DIM)
     values_full = values_all[0].reshape(length, HEADS, HEAD_DIM)

time: 709 us -> 660 us (0.931)
  waiting for transfers between devices: 620 us -> 558 us
  starting transfers between devices: 4.79 us -> 15.7 us
    all_gather x1 -> x0, waiting for transfers between devices: 65.9 us -> none  [body(): lax.all_gather(value_rows, 'seq', axis=1, tiled=True)]
    all_to_all x0 -> x1, waiting for transfers between devices: none -> 32.7 us  [body(): lax.all_to_all(jnp.stack([value_rows] * lax.axis_size('seq')), 'seq', 0, 0)]
    all_gather x1, waiting for transfers between devices: 71 us -> 42 us  [body(): lax.all_gather(key_rows, 'seq', axis=1, tiled=True)]
    all_to_all x0 -> x1, starting transfers between devices: none -> 10.9 us  [body(): lax.all_to_all(jnp.stack([value_rows] * lax.axis_size('seq')), 'seq', 0, 0)]
    unnamed x37 -> x43, local copies, waits for them, and re-layouts: 24.5 us -> 23.8 us
    unnamed x8 -> x7, waiting for transfers between devices: 148 us -> 148 us
  transfers between devices with their start and end apart: 9 -> 9, of which waited for: 8 -> 8; matrix products, arithmetic and copies ran while one was open for 9% -> 10% of each run, Pallas kernels for 0% -> 0%
where the time goes in v1:
time: 660 us; the launch traced here: 659 us
  waiting for transfers between devices  558 us (85%)
  local copies, waits for them, and re-layouts  39.1 us (6%)
  matrix products  27.6 us (4%)
  starting transfers between devices  15.7 us (2%)
  between operations  14.5 us (2%)
    unnamed x7, waiting for transfers between devices  148 us
    psum x1, waiting for transfers between devices, body(): summed = lax.psum(owned, 'seq')  125 us
    reduce_scatter x1, waiting for transfers between devices, body(): lax.psum_scatter(value_part.reshape(1, length, channels).astype(jnp.bfloa...  92.6 us
    reduce_scatter x1, waiting for transfers between devices, body(): lax.psum_scatter(key_part.reshape(1, length, channels).astype(jnp.bfloat1...  90.7 us
    all_gather x1, waiting for transfers between devices, body(): lax.all_gather(key_rows, 'seq', axis=1, tiled=True)  42 us
    all_to_all x1, waiting for transfers between devices, body(): lax.all_to_all(jnp.stack([value_rows] * lax.axis_size('seq')), 'seq', 0, 0)  32.7 us
    all_gather x1, waiting for transfers between devices, body(): full_weight = lax.all_gather(conv_weight, 'dp', axis=0, tiled=True)  23.9 us
    unnamed x43, local copies, waits for them, and re-layouts  23.8 us
  transfers between devices with their start and end apart: 9, of which 8 were waited for; matrix products, arithmetic and copies ran while one was open for 10% of the time, Pallas kernels for 0%

profile of v1, /device:TPU:8, one launch (start us, length us, event | category | flops | bytes accessed | tf_op | source)
XLA Modules:
  0.0 659.4 jit_solution(12837300147549064163)
XLA Ops:
  9.8 1.4 stack.16
  11.1 10.9 %all-to-all-start = ((bf16[8,1,128,768]{2,3,1,0:T(8,128)(2,1)}), bf16[8,1,128,768]{2,3,1,0:T(8,128)(2,1)S(1)}, u32[]{:S(2)}, u32[]{:S(2)}) async-start(bf16[8,1,128,768]{2,3,1,0:T(8,128)(2,1)} %stack.16), calls=%async_computation | async-start | bytes 3145728 | tf_op jit(solution)/shard_map/all_to_all | solution.py:64
  23.2 32.7 %all-to-all-done = bf16[8,1,128,768]{2,3,1,0:T(8,128)(2,1)S(1)} async-done(((bf16[8,1,128,768]{2,3,1,0:T(8,128)(2,1)}), bf16[8,1,128,768]{2,3,1,0:T(8,128)(2,1)S(1)}, u32[]{:S(2)}, u32[]{:S(2)}) %all-to-all-start) | async-done | bytes 1572896 | tf_op jit(solution)/shard_map/all_to_all | solution.py:64
  57.0 2.1 reshape_squeeze_reshape.3
  59.0 42.0 %all-gather.3.cloned.1.call-done = bf16[1,1024,768]{2,1,0:T(8,128)(2,1)} async-done(((bf16[1,128,768]{2,1,0:T(8,128)(2,1)}), bf16[1,1024,768]{2,1,0:T(8,128)(2,1)}) %all-gather.3.cloned.1.call-update) | async-done | bytes 1572880 | tf_op jit(solution)/shard_map/all_gather | solution.py:62
  101.0 1.7 copy.36
  104.5 1.7 copy-done.11
  108.0 3.0 collective-permute-start.1
  111.0 1.3 collective-permute-start
  112.4 4.2 collective-permute-done
  120.3 1.6 copy.45
  121.9 6.0 convolution_bitcast_fusion
  127.9 12.5 %copy.48 = f32[768,3840]{1,0:T(8,128)} copy(f32[768,3840]{0,1:T(8,128)} %convolution_bitcast_fusion) | data formatting | bytes 23592960
  140.7 23.9 %all-gather.5.cloned.1.call-done = bf16[768,5,768]{2,0,1:T(8,128)(2,1)} async-done(((bf16[24,5,768]{2,0,1:T(8,128)(2,1)}), bf16[768,5,768]{2,0,1:T(8,128)(2,1)}) %all-gather.5.cloned.1.call-update) | async-done | bytes 5898256 | tf_op jit(solution)/shard_map/all_gather | solution.py:74
  164.6 1.6 fusion.15
  166.2 1.6 convolution_add_fusion.3
  167.8 1.6 convolution_add_fusion.2
  169.4 1.6 convolution_add_fusion.1
  171.0 1.9 fusion.41
  173.3 146.1 %reduce-scatter.10.cloned.1.call-done = f32[24,3840]{1,0:T(8,128)} async-done(((f32[768,3840]{1,0:T(8,128)}), f32[24,3840]{1,0:T(8,128)}) %reduce-scatter.10.cloned.1.call-update) | async-done | bytes 368656
  319.4 2.8 copy.49
  322.5 4.6 fusion.9
  327.1 2.7 copy.44
  330.9 3.9 multiply_convert_fusion
  334.8 1.3 copy-done.1
  336.7 1.7 copy.43
  338.4 2.4 fusion.16
  341.6 124.6 %all-reduce.2.cloned.1.call-done = f32[24,3840]{0,1:T(8,128)} async-done(((f32[24,3840]{0,1:T(8,128)}), f32[24,3840]{0,1:T(8,128)}) %all-reduce.2.cloned.1.call-update) | async-done | bytes 368656 | tf_op jit(solution)/shard_map/psum | solution.py:89
  466.2 1.7 broadcast_multiply_fusion
  467.9 1.3 copy.47
  469.2 92.6 %reduce-scatter.8.cloned.1.call-done = bf16[1,128,768]{2,1,0:T(8,128)(2,1)} async-done(((bf16[1,1024,768]{2,1,0:T(8,128)(2,1)}), bf16[1,128,768]{2,1,0:T(8,128)(2,1)}) %reduce-scatter.8.cloned.1.call-update) | async-done | bytes 196624 | tf_op jit(solution)/shard_map/reduce_scatter | solution.py:115
  561.8 90.7 %reduce-scatter.6.cloned.1.call-done = bf16[1,128,768]{2,1,0:T(8,128)(2,1)} async-done(((bf16[1,1024,768]{2,1,0:T(8,128)(2,1)}), bf16[1,128,768]{2,1,0:T(8,128)(2,1)}) %reduce-scatter.6.cloned.1.call-update) | async-done | bytes 196624 | tf_op jit(solution)/shard_map/reduce_scatter | solution.py:109
  (70 shorter events, 15.2 us)
Async XLA Ops:
  7.2 14.9 %copy-start.16 = (bf16[1,128,768]{2,1,0:T(8,128)(2,1)S(1)}, bf16[1,128,768]{2,1,0:T(8,128)(2,1)}, u32[]{:S(2)}) copy-start(bf16[1,128,768]{2,1,0:T(8,128)(2,1)} %param.7) | copy-start | bytes 589828
  7.2 15.1 %copy-start.9 = (bf16[1,128,768]{2,1,0:T(8,128)(2,1)S(1)}, bf16[1,128,768]{2,1,0:T(8,128)(2,1)}, u32[]{:S(2)}) copy-start(bf16[1,128,768]{2,1,0:T(8,128)(2,1)} %param.6) | copy-start | bytes 589828
  7.2 93.8 %all-gather.3.cloned.1.call-start = ((), (), s32[]{:S(2)}) async-start(), calls=%async_computation.4 | async-start | bytes 1769472 | tf_op jit(solution)/shard_map/all_gather | solution.py:62
  7.9 156.6 %all-gather.5.cloned.1.call-start = ((), (), s32[]{:S(2)}) async-start(), calls=%async_computation.5 | async-start | bytes 6082560 | tf_op jit(solution)/shard_map/all_gather | solution.py:74
  11.1 44.8 %all-to-all-start = ((bf16[8,1,128,768]{2,3,1,0:T(8,128)(2,1)}), bf16[8,1,128,768]{2,3,1,0:T(8,128)(2,1)S(1)}, u32[]{:S(2)}, u32[]{:S(2)}) async-start(bf16[8,1,128,768]{2,3,1,0:T(8,128)(2,1)} %stack.16), calls=%async_computation | async-start | bytes 3145728 | tf_op jit(solution)/shard_map/all_to_all | solution.py:64
  22.1 297.3 %reduce-scatter.10.cloned.1.call-start = ((), (), s32[]{:S(2)}) async-start(), calls=%async_computation.9 | async-start | bytes 12165120
  22.3 80.5 %copy-start.7 = (bf16[1,128,768]{1,2,0:T(8,128)(2,1)}, bf16[1,128,768]{1,2,0:T(8,128)(2,1)S(1)}, u32[]{:S(2)}) copy-start(bf16[1,128,768]{1,2,0:T(8,128)(2,1)S(1)} %copy.35) | copy-start | bytes 589828
  103.6 3.9 copy-start
  103.6 2.6 copy-start.11
  103.6 2.9 copy-start.15
  106.5 1.2 copy-start.10
  106.5 1.4 copy-start.2
  108.0 4.4 collective-permute-start.1
  111.0 5.5 collective-permute-start
  116.7 2.9 copy-start.3
  116.7 2.9 copy-start.5
  140.4 24.2 %copy-start.6 = (bf16[2,130,768]{2,1,0:T(8,128)(2,1)S(1)}, bf16[2,130,768]{2,1,0:T(8,128)(2,1)}, u32[]{:S(2)}) copy-start(bf16[2,130,768]{2,1,0:T(8,128)(2,1)} %copy-done.5) | copy-start | bytes 1198084
  140.4 325.8 %all-reduce.2.cloned.1.call-start = ((), (), s32[]{:S(2)}) async-start(), calls=%async_computation.8 | async-start | bytes 3932160 | tf_op jit(solution)/shard_map/psum | solution.py:89
  140.7 28.7 %copy-start.4 = (bf16[2,130,768]{2,1,0:T(8,128)(2,1)S(1)}, bf16[2,130,768]{2,1,0:T(8,128)(2,1)}, u32[]{:S(2)}) copy-start(bf16[2,130,768]{2,1,0:T(8,128)(2,1)} %copy-done.3) | copy-start | bytes 1198084
  173.1 149.4 %copy-start.13 = (bf16[128,768]{1,0:T(8,128)(2,1)}, bf16[128,768]{1,0:T(8,128)(2,1)S(1)}, u32[]{:S(2)}) copy-start(bf16[128,768]{1,0:T(8,128)(2,1)S(1)} %fusion.43) | copy-start | bytes 589828
  173.3 149.2 %copy-start.14 = (bf16[128,768]{0,1:T(8,128)(2,1)}, bf16[128,768]{0,1:T(8,128)(2,1)S(1)}, u32[]{:S(2)}) copy-start(bf16[128,768]{0,1:T(8,128)(2,1)S(1)} %copy.42) | copy-start | bytes 589828
  322.2 239.6 %reduce-scatter.8.cloned.1.call-start = ((), (), s32[]{:S(2)}) async-start(), calls=%async_computation.7 | async-start | bytes 1769472 | tf_op jit(solution)/shard_map/reduce_scatter | solution.py:115
  327.1 3.7 copy-start.12
  329.8 322.7 %reduce-scatter.6.cloned.1.call-start = ((), (), s32[]{:S(2)}) async-start(), calls=%async_computation.6 | async-start | bytes 1769472 | tf_op jit(solution)/shard_map/reduce_scatter | solution.py:109
  330.9 5.3 copy-start.8
  334.8 1.3 copy-start.1
Sparse Core Ops, SparseCore 0:
  10.6 90.3 all-gather.2
  102.8 61.6 all-gather.4
  167.1 152.2 reduce-scatter.9
  322.4 143.7 all-reduce.1
  470.7 91.1 reduce-scatter.7
  566.3 86.1 reduce-scatter.5
